TPU v7x, 512 devices: a whole 4x8x8 slice. The times are simulated.
512 devices in a mesh: dp: 8 (over x, z_lo), fsdp: 64 (over z_hi, y, core).
Axes of the slice: x: 4, y: 8, z: 8 (z_hi: 4, z_lo: 2; z = z_hi * 2 + z_lo), core: 2. Of those that a mesh axis runs over, the one named last changes fastest.
Arguments:
- tokens: bfloat16 [512, 256, 3584], P(('dp', 'fsdp')), may hold values from -11 to 11
- queries: bfloat16 [512, 256, 1792], P(('dp', 'fsdp')), may hold values from -48 to 48
- key_weight: bfloat16 [3584, 256], P('fsdp'), may hold values from -0.09375 to 0.09375
- value_weight: bfloat16 [3584, 256], P('fsdp'), may hold values from -0.09375 to 0.09375
- key_variance: float32 [3584, 256], P('fsdp'), may hold values from 0.00069754466 to 0.013950893
- sign_bits: int32 [3584, 35], P('fsdp'), may hold values from 0 to 1073741823
Outputs:
- attended: bfloat16 [512, 256, 1792], P(('dp', 'fsdp'))
- spread: bfloat16 [512, 256, 1792], P(('dp', 'fsdp'))
- head_mean: float32 [14], replicated
All inputs are finite; a program needn't handle non-finite values.
Results may differ from a plain program's by a relative error of at most 0.014.
The roundings to bfloat16 on the way count: a program that leaves them out, or rounds other values in their place, can miss the bound.
Values may be sent and summed in bfloat16 or wider, within the bound.
A program may use at most 128 MiB of HBM per device.

v0:
```python
import jax
import jax.numpy as jnp
import numpy as np
from jax import lax
from jax.sharding import Mesh
from jax.sharding import PartitionSpec as P

HD = 128
KVH = 2
QPK = 7
TANG = 4
FSDP = ("fsdp_0", "fsdp_1", "fsdp_2")
DP_FSDP = ("dp_0", "dp_1", "fsdp_0", "fsdp_1", "fsdp_2")
DP = ("dp_0", "dp_1")


word_bits = 30


def laid_out(pieces, dim):
    shape = list(pieces.shape[1:])
    shape[dim] *= pieces.shape[0]
    return jnp.moveaxis(pieces, 0, dim).reshape(shape)


def from_everyone(shard, axis):
    copies = jnp.broadcast_to(shard, (lax.axis_size(axis), *shard.shape))
    return lax.all_to_all(copies, axis, split_axis=0, concat_axis=0, tiled=True)


def collect(shard, axis, dim):
    return laid_out(from_everyone(shard, axis), dim)


def sent_together(arrays, axis, dim, along):
    ends, at = ([], 0)
    for a in arrays[:-1]:
        at += a.shape[along]
        ends.append(at)
    both = jnp.concatenate(arrays, axis=along)
    return tuple(jnp.split(lax.all_gather(both, axis, axis=dim, tiled=True), ends, axis=along))


def by_axis(shard, axes):
    for axis in axes:
        shard = lax.psum(shard, axis)
    return shard


def sign_table(packed, columns):
    position = np.arange(columns)
    chosen = jnp.take(packed, jnp.asarray(position // word_bits, jnp.int32), axis=1)
    shifted = jnp.right_shift(chosen, jnp.asarray(position % word_bits, jnp.int32))
    return (2 * jnp.bitwise_and(shifted, 1) - 1).astype(jnp.float32)


def scaled_rows(root_rows, packed_rows):
    tiled = jnp.tile(root_rows, (1, TANG)).astype(jnp.float32)
    return (tiled * sign_table(packed_rows, TANG * root_rows.shape[1])).astype(jnp.bfloat16)


def attend(query_rows, key_rows, value_rows, tangent_keys):
    length = query_rows.shape[0]
    factor = HD ** (-0.5)
    causal = jnp.arange(length)[:, None] >= jnp.arange(length)[None, :]
    outputs = []
    spreads = []
    tangent_split = tangent_keys.reshape(length, TANG, KVH, HD)
    for group in range(KVH):
        query_group = query_rows[:, group * QPK * HD : (group + 1) * QPK * HD].reshape(
            length, QPK, HD
        )
        key_group = key_rows[:, group * HD : (group + 1) * HD]
        value_group = value_rows[:, group * HD : (group + 1) * HD]
        tangent_group = tangent_split[:, :, group, :]
        scores = (
            jnp.einsum("qhd,kd->hqk", query_group, key_group, preferred_element_type=jnp.float32)
            * factor
        )
        scores = jnp.where(causal, scores, -jnp.inf)
        raised = jnp.exp(scores - jnp.max(scores, axis=-1, keepdims=True))
        weights = raised / jnp.sum(raised, axis=-1, keepdims=True)
        rounded = weights.astype(jnp.bfloat16)
        outputs.append(
            jnp.einsum(
                "hqk,kd->qhd", rounded, value_group, preferred_element_type=jnp.float32
            ).reshape(length, QPK * HD)
        )
        moved = (
            jnp.einsum(
                "qhd,ktd->thqk", query_group, tangent_group, preferred_element_type=jnp.float32
            )
            * factor
        )
        centred = weights * (moved - jnp.sum(weights * moved, axis=-1, keepdims=True))
        response = jnp.einsum(
            "thqk,kd->tqhd",
            centred.astype(jnp.bfloat16),
            value_group,
            preferred_element_type=jnp.float32,
        )
        spreads.append((jnp.sum(response * response, axis=0) / TANG).reshape(length, QPK * HD))
    return (jnp.concatenate(outputs, axis=1), jnp.concatenate(spreads, axis=1))


def body(tokens, queries, key_weight, value_weight, key_variance, sign_bits):
    token_rows = tokens[0]
    length = token_rows.shape[0]
    root = jnp.sqrt(key_variance).astype(jnp.bfloat16)
    all_words = collect(sign_bits, FSDP, 0)
    pieces = sent_together((key_weight, value_weight, root), FSDP, 0, 1)
    built = scaled_rows(pieces[2], all_words)
    key_sum = jnp.dot(token_rows, pieces[0], preferred_element_type=jnp.float32)
    value_sum = jnp.dot(token_rows, pieces[1], preferred_element_type=jnp.float32)
    tangent_sum = jnp.dot(token_rows, built, preferred_element_type=jnp.float32)
    key_rows = key_sum.astype(jnp.bfloat16)
    value_rows = value_sum.astype(jnp.bfloat16)
    tangent_keys = tangent_sum.astype(jnp.bfloat16)
    attended, variance = attend(queries[0], key_rows, value_rows, tangent_keys)
    local_sums = jnp.sum(variance.reshape(length, -1, HD), axis=(0, 2))
    totals = by_axis(local_sums, DP_FSDP)
    count = lax.axis_size(DP) * lax.axis_size(FSDP) * length * HD
    head_mean = totals / count
    return (attended.astype(jnp.bfloat16)[None], variance.astype(jnp.bfloat16)[None], head_mean)


def solution(mesh):
    torus = Mesh(
        mesh.devices.reshape(4, 2, 4, 8, 2), ("dp_0", "dp_1", "fsdp_0", "fsdp_1", "fsdp_2")
    )
    placed = (
        P(DP_FSDP, None, None),
        P(DP_FSDP, None, None),
        P(FSDP, None),
        P(FSDP, None),
        P(FSDP, None),
        P(FSDP, None),
    )
    return jax.shard_map(
        body,
        mesh=torus,
        in_specs=placed,
        out_specs=(P(DP_FSDP, None, None), P(DP_FSDP, None, None), P()),
        check_vma=False,
    )
```

profile of v0, /device:TPU:1, one launch (start us, length us, event | category | flops | bytes accessed | tf_op | source)
XLA Modules:
  0.0 218.4 jit_solution(2104663565856342874)
XLA Ops:
  7.2 0.0 all-gather.2.cloned.1.call-start
  7.2 1.0 sqrt_convert_fusion
  8.2 1.4 pad_maximum_fusion.2
  9.6 0.8 broadcast_bitcast_fusion
  10.4 2.3 %reshape.212 = s32[64,1,1960]{2,1,0:T(1,128)} reshape(s32[64,35,56]{2,1,0:T(8,128)S(1)} %broadcast_bitcast_fusion) | data formatting | bytes 1003520
  12.7 17.8 %all-to-all-start = ((s32[64,1,1960]{2,1,0:T(1,128)}), s32[64,1,1960]{2,1,0:T(1,128)S(1)}, u32[]{:S(2)}, u32[]{:S(2)}) async-start(s32[64,1,1960]{2,1,0:T(1,128)} %reshape.212), calls=%async_computation | async-start | bytes 1048576 | tf_op jit(solution)/shard_map/all_to_all | solution.py:28
  30.5 1.5 copy.39
  32.0 1.0 fusion.87
  33.0 17.1 %all-to-all-done = s32[64,1,1960]{2,1,0:T(1,128)S(1)} async-done(((s32[64,1,1960]{2,1,0:T(1,128)}), s32[64,1,1960]{2,1,0:T(1,128)S(1)}, u32[]{:S(2)}, u32[]{:S(2)}) %all-to-all-start) | async-done | bytes 501792 | tf_op jit(solution)/shard_map/all_to_all | solution.py:28
  50.1 0.5 broadcast.189
  50.7 2.8 %reduce.2 = s32[64,1960]{1,0:T(8,128)} reduce(s32[64,1,1960]{2,1,0:T(1,128)S(1)} %all-to-all-done, s32[]{:T(128)} %broadcast.189), dimensions={1}, to_apply=%all_to_all.3.reduce_sub_computation | reduce | bytes 1003524 | tf_op jit(solution)/shard_map/all_to_all | solution.py:28
  53.4 1.6 reshape.213
  55.0 1.2 copy.49
  56.2 1.9 reshape.192
  58.2 8.9 %gather_fusion = s32[1024,3584]{1,0:T(8,128)} fusion(s32[3584,35]{0,1:T(8,128)S(1)} %reshape.192, s32[1024]{0:T(1024)S(1)} %broadcast_clamp_fusion), kind=kCustom, calls=%fused_computation | custom fusion | bytes 29364224 | tf_op jit(solution)/shard_map/jit(_take)/gather | solution.py:52
  67.0 48.5 %all-gather.2.cloned.1.call-done = bf16[3584,768]{1,0:T(8,128)(2,1)} async-done(((bf16[56,768]{1,0:T(8,128)(2,1)}), bf16[3584,768]{1,0:T(8,128)(2,1)}) %all-gather.2.cloned.1.call-update) | async-done | bytes 5505040 | tf_op jit(solution)/shard_map/all_gather | solution.py:41
  115.5 3.7 %slice_convert_fusion = f32[3584,256]{1,0:T(8,128)} fusion(bf16[3584,768]{1,0:T(8,128)(2,1)} %all-gather.2.cloned.1.call-done), kind=kLoop, calls=%fused_computation.26 | loop fusion | flops 917504 | bytes 5505024 | tf_op jit(solution)/shard_map/convert_element_type | solution.py:58
  119.2 5.1 %copy.48 = f32[3584,256]{0,1:T(8,128)} copy(f32[3584,256]{1,0:T(8,128)} %slice_convert_fusion) | data formatting | bytes 7340032 | tf_op jit(solution)/shard_map/convert_element_type | solution.py:58
  124.3 2.2 %fusion.47 = bf16[256,256]{0,1:T(8,128)(2,1)S(1)} fusion(bf16[1,256,3584]{2,1,0:T(8,128)(2,1)S(1)} %copy-done, bf16[3584,768]{1,0:T(8,128)(2,1)} %all-gather.2.cloned.1.call-done), kind=kOutput, calls=%fused_computation.47 | convolution fusion | flops 469827584 | bytes 3801088 | tf_op jit(solution)/shard_map/dot_general | solution.py:113
  126.6 1.9 fusion.88
  128.5 2.0 fusion.89
  130.5 3.2 %broadcast_multiply_fusion.1 = (f32[7,256,256]{1,2,0:T(8,128)}, f32[7,256,256]{1,2,0:T(8,128)S(1)}) fusion(f32[7,256,256]{1,2,0:T(8,128)} %get-tuple-element.22, f32[7,256]{1,0:T(8,128)S(1)} %get-tuple-element.21), kind=kLoop, calls=%fused_computation.52 | loop fusion | flops 917504 | bytes 5512192 | tf_op jit(solution)/shard_map/mul | solution.py:95
  133.6 2.8 %fusion.52 = bf16[256,256]{0,1:T(8,128)(2,1)S(1)} fusion(bf16[1,256,3584]{2,1,0:T(8,128)(2,1)S(1)} %copy-done, bf16[3584,768]{1,0:T(8,128)(2,1)} %all-gather.2.cloned.1.call-done), kind=kOutput, calls=%fused_computation.48 | convolution fusion | flops 469827584 | bytes 3801088 | tf_op jit(solution)/shard_map/dot_general | solution.py:114
  136.5 0.3 convolution_convert_fusion.1
  136.8 1.0 copy.46
  137.8 3.1 %broadcast_multiply_fusion = (f32[7,256,256]{1,2,0:T(8,128)}, f32[7,256,256]{1,2,0:T(8,128)S(1)}) fusion(f32[7,256,256]{1,2,0:T(8,128)} %get-tuple-element.20, f32[7,256]{1,0:T(8,128)S(1)} %get-tuple-element.19), kind=kLoop, calls=%fused_computation.51 | loop fusion | flops 917504 | bytes 5512192 | tf_op jit(solution)/shard_map/mul | solution.py:95
  140.9 1.2 copy-done.1
  142.1 0.3 convolution_convert_fusion
  142.4 1.0 copy.47
  143.4 8.0 %multiply_convert_fusion = bf16[3584,4,256]{0,2,1:T(8,128)(2,1)S(1)} fusion(s32[3584,4,256]{0,2,1:T(8,128)} %bitcast.155, s32[4,256]{1,0:T(4,128)S(1)} %copy-done.11, f32[3584,256]{0,1:T(8,128)} %copy.48), kind=kLoop, calls=%fused_computation.3 | loop fusion | flops 25690112 | bytes 25694208 | tf_op jit(solution)/shard_map/convert_element_type | solution.py:59
  151.5 2.1 fusion.30
  153.6 1.2 fusion.9
  154.8 0.3 copy-done.4
  155.1 1.6 multiply_reduce_fusion.1
  156.7 1.2 fusion.5
  157.9 0.3 copy-done.2
  158.2 1.6 multiply_reduce_fusion
  159.8 1.0 multiply_bitcast_fusion
  160.8 0.2 maximum_reduce_fusion
  161.0 8.4 %psum.35 = f32[14]{0:T(128)S(1)} all-reduce(f32[14]{0:T(128)S(1)} %maximum_reduce_fusion), channel_id=1, replica_groups=mesh['dp_0'=4,'dp_1'=2,'fsdp_0'=4,'fsdp_1'=8,'fsdp_2'=2] {'dp_0'}, use_global_device_ids=true, to_apply=%region_9.10 | all-reduce | flops 14 | bytes 112 | tf_op jit(solution)/shard_map/psum | solution.py:46
  169.4 3.8 %psum.36 = f32[14]{0:T(128)S(1)} all-reduce(f32[14]{0:T(128)S(1)} %psum.35), channel_id=1, replica_groups=mesh['dp_0'=4,'dp_1'=2,'fsdp_0'=4,'fsdp_1'=8,'fsdp_2'=2] {'dp_1'}, use_global_device_ids=true, to_apply=%region_10.11 | all-reduce | flops 14 | bytes 112 | tf_op jit(solution)/shard_map/psum | solution.py:46
  173.2 9.2 %psum.37 = f32[14]{0:T(128)S(1)} all-reduce(f32[14]{0:T(128)S(1)} %psum.36), channel_id=1, replica_groups=mesh['dp_0'=4,'dp_1'=2,'fsdp_0'=4,'fsdp_1'=8,'fsdp_2'=2] {'fsdp_0'}, use_global_device_ids=true, to_apply=%region_11.12 | all-reduce | flops 14 | bytes 112 | tf_op jit(solution)/shard_map/psum | solution.py:46
  182.4 13.0 %psum.38 = f32[14]{0:T(128)S(1)} all-reduce(f32[14]{0:T(128)S(1)} %psum.37), channel_id=1, replica_groups=mesh['dp_0'=4,'dp_1'=2,'fsdp_0'=4,'fsdp_1'=8,'fsdp_2'=2] {'fsdp_1'}, use_global_device_ids=true, to_apply=%region_12.13 | all-reduce | flops 14 | bytes 112 | tf_op jit(solution)/shard_map/psum | solution.py:46
  195.3 11.2 %psum.39 = f32[14]{0:T(128)S(1)} all-reduce(f32[14]{0:T(128)S(1)} %psum.38), channel_id=1, replica_groups=mesh['dp_0'=4,'dp_1'=2,'fsdp_0'=4,'fsdp_1'=8,'fsdp_2'=2] {'fsdp_2'}, use_global_device_ids=true, to_apply=%region_13.14 | all-reduce | flops 14 | bytes 112 | tf_op jit(solution)/shard_map/psum | solution.py:46
  206.6 0.5 broadcast_multiply_fusion.2
  207.1 1.1 pad_maximum_fusion.1
  208.2 1.4 copy.56
  209.6 2.0 pad_maximum_fusion
  (24 shorter events, 0.1 us)
Async XLA Ops:
  7.2 117.1 %copy-start = (bf16[1,256,3584]{2,1,0:T(8,128)(2,1)S(1)}, bf16[1,256,3584]{2,1,0:T(8,128)(2,1)}, u32[]{:S(2)}) copy-start(bf16[1,256,3584]{2,1,0:T(8,128)(2,1)} %param.8) | copy-start | bytes 5505028
  7.2 108.3 %all-gather.2.cloned.1.call-start = ((), (), s32[]{:S(2)}) async-start(), calls=%async_computation.1 | async-start | bytes 5591040 | tf_op jit(solution)/shard_map/all_gather | solution.py:41
  12.7 19.3 %copy-start.10 = (s32[1024]{0:T(1024)S(1)}, s32[1024]{0:T(1024)}, u32[]{:S(2)}) copy-start(s32[1024]{0:T(1024)} %constant.58) | copy-start | bytes 12292
  12.7 37.4 %all-to-all-start = ((s32[64,1,1960]{2,1,0:T(1,128)}), s32[64,1,1960]{2,1,0:T(1,128)S(1)}, u32[]{:S(2)}, u32[]{:S(2)}) async-start(s32[64,1,1960]{2,1,0:T(1,128)} %reshape.212), calls=%async_computation | async-start | bytes 1048576 | tf_op jit(solution)/shard_map/all_to_all | solution.py:28
  124.3 2.3 %copy-start.8 = (bf16[256,896]{0,1:T(8,128)(2,1)S(1)}, bf16[256,896]{0,1:T(8,128)(2,1)}, u32[]{:S(2)}) copy-start(bf16[256,896]{0,1:T(8,128)(2,1)} %get-tuple-element.18) | copy-start | bytes 1376260
  126.5 1.9 copy-start.9
  133.6 2.9 %copy-start.3 = (f32[7,256,256]{1,2,0:T(8,128)}, f32[7,256,256]{1,2,0:T(8,128)S(1)}, u32[]{:S(2)}) copy-start(f32[7,256,256]{1,2,0:T(8,128)S(1)} %get-tuple-element.10) | copy-start | bytes 5505028
  140.9 1.2 copy-start.1
  140.9 2.5 %copy-start.11 = (s32[4,256]{1,0:T(4,128)S(1)}, s32[4,256]{1,0:T(4,128)}, u32[]{:S(2)}) copy-start(s32[4,256]{1,0:T(4,128)} %constant.56) | copy-start | bytes 12292
  151.5 2.1 copy-start.5
  153.6 1.5 copy-start.4
  155.1 1.6 copy-start.6
  156.7 1.5 copy-start.2
  208.2 1.4 copy-start.7
Sparse Core Ops, SparseCore 0:
  11.3 104.2 all-gather.1
where the time goes:
time: 219 us; the launch traced here: 218 us
  waiting for transfers between devices  65.6 us (30%)
  blocking collectives  45.6 us (21%)
  local copies, waits for them, and re-layouts  30 us (14%)
  other arithmetic  27.9 us (13%)
  starting transfers between devices  17.8 us (8%)
  matrix products  17.2 us (8%)
  between operations  14.3 us (7%)
    all_gather x1, waiting for transfers between devices, sent_together(): lax.all_gather(both, axis, axis=dim, tiled=True)  48.5 us
    psum x5, blocking collectives, by_axis(): shard = lax.psum(shard, axis)  45.6 us
    all_to_all x1, starting transfers between devices, from_everyone(): return lax.all_to_all(copies, axis, split_axis=0, concat_axis=0, tiled=True)  17.8 us
    all_to_all x1, waiting for transfers between devices, from_everyone(): return lax.all_to_all(copies, axis, split_axis=0, concat_axis=0, tiled=True)  17.1 us
    unnamed x29, local copies, waits for them, and re-layouts  9.42 us
    gather x1, local copies, waits for them, and re-layouts, sign_table(): jnp.take(packed, jnp.asarray(position // word_bits, jnp.int32), axis=1)  8.86 us
    convert_element_type x1, other arithmetic, scaled_rows(): (tiled * sign_table(packed_rows, TANG * root_rows.shape[1])).astype(jnp.b...  8.02 us
    mul x2, other arithmetic, attend(): weights * moved  6.26 us
  transfers between devices with their start and end apart: 2, of which 2 were waited for; matrix products, arithmetic and copies ran while one was open for 10% of the time, Pallas kernels for 0%

commit v1 on v0

v1 whole, which is shorter than its diff:
```python
import functools

import jax
import jax.numpy as jnp
from jax import lax
from jax.experimental import pallas as pl
from jax.experimental.pallas import tpu as pltpu
from jax.sharding import Mesh
from jax.sharding import PartitionSpec as P

HD = 128
KVH = 2
QPK = 7
TANG = 4
HEADS = KVH * QPK
LEN = 256
D = 3584
KVW = KVH * HD
HALF = 3 * HD
WORD_BITS = 30
WORDS = 35
SHARD = 56
WROWS = 24
WLANES = 40
MESH = pl.DeviceIdType.MESH
FSDP = ("fsdp_0", "fsdp_1", "fsdp_2")
ALL = ("dp_0", "dp_1", "fsdp_0", "fsdp_1", "fsdp_2")

SPLIT = ((0, -1), (-2, 1), (2, -3), (4, 3))


def gather_kernel(
    key_ref, value_ref, var_ref, bits_ref,
    buf_a, buf_b, buf_w,
    own_a, own_b, own_w, wide,
    send_a, send_b, send_w, recv_a, recv_b, recv_w, sib_a, sib_b, sib_w, local,
):
    zl = lax.axis_index("dp_1")
    zh = lax.axis_index("fsdp_0")
    y = lax.axis_index("fsdp_1")
    c = lax.axis_index("fsdp_2")
    side = 2 * zl - 1
    g1 = lax.rem(zh + side + 4, 4)
    g2 = lax.rem(zh - side + 4, 4)
    g3 = lax.rem(zh + 2, 4)
    up = {"fsdp_1": lax.rem(y + 1, 8)}
    down = {"fsdp_1": lax.rem(y + 7, 8)}
    near = {"dp_1": 1 - zl, "fsdp_0": g1}
    far = {"dp_1": 1 - zl}
    twin = {"fsdp_2": 1 - c}
    barrier = pltpu.get_barrier_semaphore()
    for peer in (up, down, near, far, twin):
        pl.semaphore_signal(barrier, inc=1, device_id=peer, device_id_type=MESH)

    own_a[:, :KVW] = jnp.sqrt(var_ref[...]).astype(jnp.bfloat16)
    own_a[:, KVW:] = key_ref[:, :HD]
    own_b[:, :HD] = key_ref[:, HD:]
    own_b[:, HD:] = value_ref[...]
    wide[...] = jnp.zeros_like(wide)
    wide[:, :WORDS] = bits_ref[...]
    spread = wide[0:24, :] + pltpu.roll(wide[24:48, :], WLANES, 1)
    own_w[...] = spread
    own_w[0:8, :] = spread[0:8, :] + pltpu.roll(wide[48:56, :], 2 * WLANES, 1)
    pl.semaphore_wait(barrier, 5)

    kinds = {
        "a": (buf_a, own_a, SHARD, send_a, recv_a, sib_a),
        "b": (buf_b, own_b, SHARD, send_b, recv_b, sib_b),
        "w": (buf_w, own_w, WROWS, send_w, recv_w, sib_w),
    }
    sent = []

    def place(kind, group, row, core):
        buf, _, size, _, _, _ = kinds[kind]
        start = pl.multiple_of((group * 16 + row * 2 + core) * size, 8)
        return buf.at[pl.ds(start, size), :]

    def push(kind, group, row, way, peer, own=False):
        _, mine, _, send, recv, sib = kinds[kind]
        slot = group * 8 + row
        there = place(kind, group, row, c)
        copy = pltpu.make_async_remote_copy(
            src_ref=mine if own else there,
            dst_ref=there,
            send_sem=send.at[way, slot],
            recv_sem=(sib if way == 3 else recv).at[slot],
            device_id=peer,
            device_id_type=MESH,
        )
        copy.start()
        sent.append(copy)

    def arrive(kind, group, row):
        _, _, _, send, recv, _ = kinds[kind]
        slot = group * 8 + row
        there = place(kind, group, row, c)
        pltpu.make_async_remote_copy(
            src_ref=there, dst_ref=there, send_sem=send.at[0, slot], recv_sem=recv.at[slot],
            device_id=twin, device_id_type=MESH,
        ).wait_recv()

    def at(offset):
        return lax.rem(y + offset + 8, 8)

    UP, DOWN, ZED, SIB = 0, 1, 2, 3
    for kind in ("a", "w", "b"):
        push(kind, zh, y, UP, up, True)
        push(kind, zh, y, DOWN, down, True)
        push(kind, zh, y, ZED, near, True)
    for kind in ("a", "w", "b"):
        push(kind, zh, y, SIB, twin, True)
    locals_ = []
    for i, kind in enumerate(("a", "b", "w")):
        copy = pltpu.make_async_copy(kinds[kind][1], place(kind, zh, y, c), local.at[i])
        copy.start()
        locals_.append(copy)

    reach = {0: (4, 3), 1: (3, 4), 2: (4, 3), 3: (3, 4)}
    groups = (zh, g1, g2, g3)
    low = lax.rem(y + zl, 2)

    def pick(pair, which):
        return pair[0] * (1 - which) + pair[1] * which

    for r in range(1, 9):
        if r <= 3:
            arrive("b", groups[r], y)
            if r == 1:
                push("b", g1, y, ZED, far)
            if r == 2:
                push("b", g2, y, ZED, near)
            push("b", groups[r], y, UP, up)
            push("b", groups[r], y, DOWN, down)
            push("b", groups[r], y, SIB, twin)
        for d, way, peer, limit, sign in ((r, UP, up, 4, -1), (r, DOWN, down, 3, 1)):
            if d <= limit:
                for kind in ("a", "w"):
                    row = at(sign * d)
                    arrive(kind, zh, row)
                    if d < limit:
                        push(kind, zh, row, way, peer)
                    push(kind, zh, row, ZED, near)
                    push(kind, zh, row, SIB, twin)
        for delay in range(4):
            d = r - delay
            if d < 1:
                continue
            for way, peer, limit, sign in ((UP, up, reach[delay][0], -1), (DOWN, down, reach[delay][1], 1)):
                if d <= limit:
                    row = at(sign * d)
                    arrive("b", groups[delay], row)
                    if d < limit:
                        push("b", groups[delay], row, way, peer)
                    push("b", groups[delay], row, SIB, twin)
        d = r - 1
        if d <= 4:
            for offset in ((0,) if d == 0 else (-4,) if d == 4 else (-d, d)):
                for kind in ("a", "w"):
                    arrive(kind, g1, at(offset))
                    push(kind, g1, at(offset), ZED, far)
                    push(kind, g1, at(offset), SIB, twin)
        if r in (4, 6):
            for pair in SPLIT[r - 4 : r - 2]:
                for onward in (True, False):
                    row = at(pick(pair, 1 - low if onward else low))
                    for kind in ("a", "w"):
                        arrive(kind, g2, row)
                        if onward:
                            push(kind, g2, row, ZED, near)
                        push(kind, g2, row, SIB, twin)
        if r in (5, 7):
            for pair in SPLIT[r - 5 : r - 3]:
                row = at(pick(pair, low))
                for kind in ("a", "w"):
                    arrive(kind, g3, row)
                    push(kind, g3, row, ZED, far)
                    push(kind, g3, row, SIB, twin)
        if r in (6, 8):
            for pair in SPLIT[r - 6 : r - 4]:
                row = at(pick(pair, 1 - low))
                for kind in ("a", "w"):
                    arrive(kind, g3, row)
                    push(kind, g3, row, SIB, twin)

    for copy in locals_:
        copy.wait()

    def last(slot, _):
        group, row = slot // 8, lax.rem(slot, 8)
        for kind in ("a", "b", "w"):
            _, _, _, send, _, sib = kinds[kind]
            there = place(kind, group, row, 1 - c)
            pltpu.make_async_remote_copy(
                src_ref=there, dst_ref=there, send_sem=send.at[0, slot], recv_sem=sib.at[slot],
                device_id=twin, device_id_type=MESH,
            ).wait_recv()
        return 0

    lax.fori_loop(0, 32, last, 0)
    for copy in sent:
        copy.wait_send()


def gather(key_weight, value_weight, key_variance, sign_bits):
    vmem = pl.BlockSpec(memory_space=pltpu.VMEM)
    return pl.pallas_call(
        gather_kernel,
        out_shape=(
            jax.ShapeDtypeStruct((D, HALF), jnp.bfloat16),
            jax.ShapeDtypeStruct((D, HALF), jnp.bfloat16),
            jax.ShapeDtypeStruct((64 * WROWS, HD), jnp.int32),
        ),
        in_specs=[vmem] * 4,
        out_specs=(vmem,) * 3,
        scratch_shapes=[
            pltpu.VMEM((SHARD, HALF), jnp.bfloat16),
            pltpu.VMEM((SHARD, HALF), jnp.bfloat16),
            pltpu.VMEM((WROWS, HD), jnp.int32),
            pltpu.VMEM((SHARD, HD), jnp.int32),
        ]
        + [pltpu.SemaphoreType.DMA((4, 32))] * 3
        + [pltpu.SemaphoreType.DMA((32,))] * 6
        + [pltpu.SemaphoreType.DMA((3,))],
        compiler_params=pltpu.CompilerParams(collective_id=0, has_side_effects=True),
        name="gather",
    )(key_weight, value_weight, key_variance, sign_bits)


def attend_kernel(
    tok_ref, query_ref, buf_a, buf_b, buf_w,
    att_ref, spread_ref, sums_ref,
    tangent, rows,
):
    lane = lax.broadcasted_iota(jnp.int32, (8, HD), 1)
    index, mask = [], []
    for k in range(8):
        column = lane + k * HD
        word = (column * 2185) >> 16
        index.append(word)
        mask.append(jnp.left_shift(jnp.ones_like(column), column - word * WORD_BITS))

    def expand(j, _):
        start = pl.multiple_of(j * 2 * SHARD, 16)
        root = buf_a[pl.ds(start, 2 * SHARD), :KVW].astype(jnp.float32)
        minus = -root
        words = buf_w[pl.ds(pl.multiple_of(j * 2 * WROWS, 8), 2 * WROWS), :]
        for k in range(8):
            cols = slice((k % 2) * HD, (k % 2 + 1) * HD)
            tiles = []
            for core in range(2):
                for rt in range(7):
                    word_tile = words[core * WROWS + (rt % 3) * 8 : core * WROWS + (rt % 3) * 8 + 8]
                    found = jnp.take_along_axis(
                        word_tile, index[k] + WLANES * (rt // 3), axis=1, mode="promise_in_bounds"
                    )
                    at = core * SHARD + rt * 8
                    tiles.append(
                        jnp.where(
                            (found & mask[k]) != 0, root[at : at + 8, cols], minus[at : at + 8, cols]
                        )
                    )
            tangent[pl.ds(start, 2 * SHARD), k * HD : (k + 1) * HD] = jnp.concatenate(
                tiles, axis=0
            ).astype(jnp.bfloat16)
        return 0

    lax.fori_loop(0, 32, expand, 0)
    keys = jnp.concatenate([buf_a[:, KVW:], buf_b[:, :HD]], axis=1)
    rows[:, :KVW] = jnp.dot(tok_ref[...], keys, preferred_element_type=jnp.float32).astype(jnp.bfloat16)
    rows[:, KVW : 2 * KVW] = jnp.dot(
        tok_ref[...], buf_b[:, HD:], preferred_element_type=jnp.float32
    ).astype(jnp.bfloat16)

    def project(t, _):
        cols = pl.ds(pl.multiple_of(t * KVW, KVW), KVW)
        out = pl.ds(pl.multiple_of(2 * KVW + t * KVW, KVW), KVW)
        rows[:, out] = jnp.dot(
            tok_ref[...], tangent[:, cols], preferred_element_type=jnp.float32
        ).astype(jnp.bfloat16)
        return 0

    lax.fori_loop(0, TANG, project, 0)
    attention(query_ref, rows, att_ref, spread_ref, sums_ref)


def attention(query_ref, rows, att_ref, spread_ref, sums_ref):
    factor = HD**-0.5
    causal = lax.broadcasted_iota(jnp.int32, (HD, HD), 0) >= lax.broadcasted_iota(jnp.int32, (HD, HD), 1)
    zeros = jnp.zeros((HD, HD), jnp.bfloat16)
    nt = (((1,), (1,)), ((), ()))

    def spread_out(top, bottom):
        top = jnp.concatenate([top.astype(jnp.bfloat16), zeros], axis=1)
        return jnp.concatenate([top, bottom.astype(jnp.bfloat16)], axis=0)

    def head(h, _):
        g = h // QPK
        cols = pl.ds(pl.multiple_of(h * HD, HD), HD)
        q = query_ref[:, cols]
        key = rows[:, pl.ds(pl.multiple_of(g * HD, HD), HD)]
        value = rows[:, pl.ds(pl.multiple_of(KVW + g * HD, HD), HD)]
        s = lax.dot_general(q, key, nt, preferred_element_type=jnp.float32)

        def soften(x):
            e = jnp.exp((x - jnp.max(x, axis=1, keepdims=True)) * factor)
            return e * (1.0 / jnp.sum(e, axis=1, keepdims=True))

        w0 = soften(jnp.where(causal, s[:HD, :HD], -jnp.inf))
        w1 = soften(
            jnp.concatenate([s[HD:, :HD], jnp.where(causal, s[HD:, HD:], -jnp.inf)], axis=1)
        )
        att_ref[:, cols] = jnp.dot(
            spread_out(w0, w1), value, preferred_element_type=jnp.float32
        ).astype(jnp.bfloat16)
        f0, f1 = w0 * factor, w1 * factor
        total = None
        for t in range(TANG):
            tk = rows[:, pl.ds(pl.multiple_of((2 + t) * KVW + g * HD, HD), HD)]
            m = lax.dot_general(q, tk, nt, preferred_element_type=jnp.float32)
            m0, m1 = m[:HD, :HD], m[HD:, :]
            c0 = f0 * (m0 - jnp.sum(w0 * m0, axis=1, keepdims=True))
            c1 = f1 * (m1 - jnp.sum(w1 * m1, axis=1, keepdims=True))
            resp = jnp.dot(spread_out(c0, c1), value, preferred_element_type=jnp.float32)
            total = resp * resp if total is None else total + resp * resp
        variance = total * (1.0 / TANG)
        spread_ref[:, cols] = variance.astype(jnp.bfloat16)
        sums_ref[h] = jnp.sum(variance.reshape(LEN // 8, 8, HD), axis=0)
        return 0

    lax.fori_loop(0, HEADS, head, 0)


def attend(tokens, queries, buf_a, buf_b, buf_w):
    vmem = pl.BlockSpec(memory_space=pltpu.VMEM)
    return pl.pallas_call(
        attend_kernel,
        out_shape=(
            jax.ShapeDtypeStruct((LEN, HEADS * HD), jnp.bfloat16),
            jax.ShapeDtypeStruct((LEN, HEADS * HD), jnp.bfloat16),
            jax.ShapeDtypeStruct((HEADS, 8, HD), jnp.float32),
        ),
        in_specs=[vmem] * 5,
        out_specs=(vmem,) * 3,
        scratch_shapes=[
            pltpu.VMEM((D, TANG * KVW), jnp.bfloat16),
            pltpu.VMEM((LEN, (2 + TANG) * KVW), jnp.bfloat16),
        ],
        compiler_params=pltpu.CompilerParams(vmem_limit_bytes=56 * 1024 * 1024),
        name="attend",
    )(tokens, queries, buf_a, buf_b, buf_w)


def reduce_kernel(count, sums_ref, out_ref, held, slots, send_sem, recv_sem):
    x = lax.axis_index("dp_0")
    zl = lax.axis_index("dp_1")
    zh = lax.axis_index("fsdp_0")
    y = lax.axis_index("fsdp_1")
    c = lax.axis_index("fsdp_2")
    mine = (zh * 2 + zl, y, x * 2 + c)

    def peer(stage, step):
        other = lax.rem(mine[stage] + step, 8)
        if stage == 0:
            return other, {"fsdp_0": other // 2, "dp_1": lax.rem(other, 2)}
        if stage == 1:
            return other, {"fsdp_1": other}
        return other, {"dp_0": other // 2, "fsdp_2": lax.rem(other, 2)}

    barrier = pltpu.get_barrier_semaphore()
    for stage in range(3):
        for step in range(1, 8):
            pl.semaphore_signal(
                barrier, inc=1, device_id=peer(stage, step)[1], device_id_type=MESH
            )
    rows = jnp.sum(jnp.sum(sums_ref[...], axis=1), axis=1, keepdims=True)
    line = lax.broadcasted_iota(jnp.int32, (HEADS, HD), 0)
    lane = lax.broadcasted_iota(jnp.int32, (HEADS, HD), 1)
    total = jnp.broadcast_to(
        jnp.sum(jnp.where(line == lane, rows, 0.0), axis=0, keepdims=True), (8, HD)
    )
    pl.semaphore_wait(barrier, 21)
    for stage in range(3):
        held[stage] = total
        slots[stage, mine[stage]] = total
        copies = []
        for step in range(1, 8):
            other, where = peer(stage, step)
            copy = pltpu.make_async_remote_copy(
                src_ref=held.at[stage],
                dst_ref=slots.at[stage, mine[stage]],
                send_sem=send_sem.at[stage, step],
                recv_sem=recv_sem.at[stage, mine[stage]],
                device_id=where,
                device_id_type=MESH,
            )
            copy.start()
            copies.append(copy)
        for step in range(1, 8):
            other, where = peer(stage, step)
            pltpu.make_async_remote_copy(
                src_ref=held.at[stage],
                dst_ref=slots.at[stage, other],
                send_sem=send_sem.at[stage, step],
                recv_sem=recv_sem.at[stage, other],
                device_id=where,
                device_id_type=MESH,
            ).wait_recv()
        total = jnp.sum(slots[stage], axis=0)
        for copy in copies:
            copy.wait_send()
    out_ref[...] = total / count


def reduce_all(sums, count):
    vmem = pl.BlockSpec(memory_space=pltpu.VMEM)
    return pl.pallas_call(
        functools.partial(reduce_kernel, count),
        out_shape=jax.ShapeDtypeStruct((8, HD), jnp.float32),
        in_specs=[vmem],
        out_specs=vmem,
        scratch_shapes=[
            pltpu.VMEM((3, 8, HD), jnp.float32),
            pltpu.VMEM((3, 8, 8, HD), jnp.float32),
            pltpu.SemaphoreType.DMA((3, 8)),
            pltpu.SemaphoreType.DMA((3, 8)),
        ],
        compiler_params=pltpu.CompilerParams(collective_id=1, has_side_effects=True),
        name="reduce",
    )(sums)


def body(tokens, queries, key_weight, value_weight, key_variance, sign_bits):
    buf_a, buf_b, buf_w = gather(key_weight, value_weight, key_variance, sign_bits)
    attended, spread, sums = attend(tokens[0], queries[0], buf_a, buf_b, buf_w)
    count = lax.axis_size(ALL) * LEN * HD
    mean = reduce_all(sums, float(count))
    return attended[None], spread[None], mean[0, :HEADS]


def solution(mesh):
    torus = Mesh(mesh.devices.reshape(4, 2, 4, 8, 2), ALL)
    placed = (P(ALL, None, None), P(ALL, None, None)) + (P(FSDP, None),) * 4
    return jax.shard_map(
        body,
        mesh=torus,
        in_specs=placed,
        out_specs=(P(ALL, None, None), P(ALL, None, None), P()),
        check_vma=False,
    )
```

time: 219 us -> 111 us (0.51)
  Pallas kernels: 0 us -> 108 us
  waiting for transfers between devices: 65.6 us -> 0 us
  blocking collectives: 45.6 us -> 0 us
  other arithmetic: 27.9 us -> 0 us
  local copies, waits for them, and re-layouts: 30 us -> 2.6 us
  starting transfers between devices: 17.8 us -> 0 us
  matrix products: 17.2 us -> 0 us
  between operations: 14.3 us -> 0.65 us
    pallas_call x0 -> x3, Pallas kernels: none -> 108 us  [the longest x1 55 us: gather(): pl.pallas_call(gather_kernel, out_shape=(jax.ShapeDtypeStruct((D, HALF),...]
    all_gather x1 -> x0, waiting for transfers between devices: 48.5 us -> none  [sent_together(): lax.all_gather(both, axis, axis=dim, tiled=True)]
    psum x5 -> x0, blocking collectives: 45.6 us -> none  [by_axis(): shard = lax.psum(shard, axis)]
    all_to_all x1 -> x0, starting transfers between devices: 17.8 us -> none  [from_everyone(): return lax.all_to_all(copies, axis, split_axis=0, concat_axis=0, tiled=True)]
    all_to_all x1 -> x0, waiting for transfers between devices: 17.1 us -> none  [from_everyone(): return lax.all_to_all(copies, axis, split_axis=0, concat_axis=0, tiled=True)]
    dot_general x9 -> x0, matrix products: 13.3 us -> none  [the longest x2 3.19 us: attend(): jnp.einsum('thqk,kd->tqhd', centred.astype(jnp.bfloat16), value_group, pr...]
    convert_element_type x3 -> x0, other arithmetic: 12.6 us -> none  [the longest x1 8.02 us: scaled_rows(): (tiled * sign_table(packed_rows, TANG * root_rows.shape[1])).astype(jnp.b...]
    gather x1 -> x0, local copies, waits for them, and re-layouts: 8.86 us -> none  [sign_table(): jnp.take(packed, jnp.asarray(position // word_bits, jnp.int32), axis=1)]
  transfers between devices with their start and end apart: 2 -> 0, of which waited for: 2 -> 0; matrix products, arithmetic and copies ran while one was open for 10% -> 0% of each run, Pallas kernels for 0% -> 0%
where the time goes in v1:
time: 111 us
  Pallas kernels  108 us (97%)
  local copies, waits for them, and re-layouts  2.6 us (2%)
    pallas_call x1, Pallas kernels, gather(): pl.pallas_call(gather_kernel, out_shape=(jax.ShapeDtypeStruct((D, HALF),...  55 us
    pallas_call x1, Pallas kernels, attend(): pl.pallas_call(attend_kernel, out_shape=(jax.ShapeDtypeStruct((LEN, HEADS...  32.9 us
    pallas_call x1, Pallas kernels, reduce_all(): pl.pallas_call(functools.partial(reduce_kernel, count), out_shape=jax.Sha...  20 us

profile of v1, /device:TPU:1, one launch (start us, length us, event | category | flops | bytes accessed | tf_op | source)
XLA Modules:
  0.0 111.1 jit_solution(3667167427301822419)
XLA Ops:
  0.6 1.4 %copy.9.bits_ref = s32[56,35]{1,0:T(8,128)} copy(s32[56,35]{0,1:T(8,128)} %param.11) | data formatting | bytes 15680 | tf_op args[5]
  2.0 55.0 %gather.1 = (bf16[3584,384]{1,0:T(8,128)(2,1)}, bf16[3584,384]{1,0:T(8,128)(2,1)}, s32[1536,128]{1,0:T(8,128)}) custom-call(bf16[56,256]{1,0:T(8,128)(2,1)} %key_ref.1, bf16[56,256]{1,0:T(8,128)(2,1)} %value_ref.1, f32[56,256]{1,0:T(8,128)} %var_ref.1, s32[56,35]{1,0:T(8,128)} %copy.9.bits_ref), custom_call_target="tpu_custom_call" | custom-call | tf_op jit(solution)/shard_map/gather/pallas_call | solution.py:206
  57.0 32.9 %attend.1 = (bf16[256,1792]{1,0:T(8,128)(2,1)}, bf16[256,1792]{1,0:T(8,128)(2,1)}, f32[14,8,128]{2,1,0:T(8,128)}) custom-call(bf16[256,3584]{1,0:T(8,128)(2,1)} %bitcast.6, bf16[256,1792]{1,0:T(8,128)(2,1)} %bitcast.7, bf16[3584,384]{1,0:T(8,128)(2,1)} %get-tuple-element.9.buf_a, bf16[3584,384]{1,0:T(8,128)(2,1)} %get-tuple-element.10.buf_b, ...), custom_call_target="tpu_custom_call" | custom-call | tf_op jit(solution)/shard_map/attend/pallas_call | solution.py:335
  89.9 20.0 %reduce.1 = f32[8,128]{1,0:T(8,128)} custom-call(f32[14,8,128]{2,1,0:T(8,128)} %get-tuple-element.14.sums_ref), custom_call_target="tpu_custom_call" | custom-call | tf_op jit(solution)/shard_map/reduce/pallas_call | solution.py:416
  109.9 1.2 %slice_bitcast_fusion = f32[14]{0:T(128)} fusion(f32[8,128]{1,0:T(8,128)} %reduce.1), kind=kLoop, calls=%fused_computation | loop fusion | bytes 112 | tf_op jit(solution)/shard_map/squeeze | solution.py:437
